TPU v7x, 32 devices: a whole 2x2x4 slice. The times are simulated.
32 devices in a mesh: dp: 16 (over z, x, core), tensor: 2 (over y).
Axes of the slice: x: 2, y: 2, z: 4, core: 2. Of those that a mesh axis runs over, the one named last changes fastest.
Arguments:
- tokens: bfloat16 [6144, 2048], P(('dp', 'tensor')), may hold values from -6 to 6
- routes: int32 [6144, 8], P('dp'), may hold values from 0 to 15, all different within a row; in each aligned block of 192 rows (0 to 191, 192 to 383, ...) at most 128 rows name the same one
- cotangent: bfloat16 [6144, 2048], P(('dp', 'tensor')), may hold values from -6 to 6
- attn_gain: float32 [2048], replicated, may hold values from 0.5 to 1.5
- q_gain: float32 [2048], replicated, may hold values from 0.5 to 1.5
- k_gain: float32 [2048], replicated, may hold values from 0.5 to 1.5
- w_query: bfloat16 [2048, 2048], P('dp', 'tensor'), may hold values from -0.125 to 0.125
- w_key: bfloat16 [2048, 2048], P('dp', 'tensor'), may hold values from -0.125 to 0.125
- w_value: bfloat16 [2048, 2048], P('dp', 'tensor'), may hold values from -0.125 to 0.125
- w_out: bfloat16 [2048, 2048], P('tensor', 'dp'), may hold values from -1 to 1
- mlp_gain: float32 [2048], replicated, may hold values from 0.5 to 1.5
- router: bfloat16 [2048, 16], replicated, may hold values from -0.0625 to 0.0625
- w_gate: bfloat16 [16, 2048, 1024], P('dp', None, 'tensor'), may hold values from -0.125 to 0.125
- w_up: bfloat16 [16, 2048, 1024], P('dp', None, 'tensor'), may hold values from -0.125 to 0.125
- w_down: bfloat16 [16, 1024, 2048], P('dp', 'tensor'), may hold values from -1.75 to 1.75
Outputs:
- layer_out: bfloat16 [6144, 2048], P(('dp', 'tensor'))
- tokens_grad: float32 [6144, 2048], P(('dp', 'tensor'))
- attn_gain_grad: float32 [2048], replicated
- q_gain_grad: float32 [2048], replicated
- k_gain_grad: float32 [2048], replicated
- w_query_grad: float32 [2048, 2048], P('dp', 'tensor')
- w_key_grad: float32 [2048, 2048], P('dp', 'tensor')
- w_value_grad: float32 [2048, 2048], P('dp', 'tensor')
- w_out_grad: float32 [2048, 2048], P('tensor', 'dp')
- mlp_gain_grad: float32 [2048], replicated
- router_grad: float32 [2048, 16], replicated
- w_gate_grad: float32 [16, 2048, 1024], P('dp', None, 'tensor')
- w_up_grad: float32 [16, 2048, 1024], P('dp', None, 'tensor')
- w_down_grad: float32 [16, 1024, 2048], P('dp', 'tensor')
Inputs may be any that keep to these rules, and one draw needn't show every extreme that they name: `routes`: each row names 8 different experts; in each aligned block of 192 rows no expert is named by more than 128 rows, and in some block one expert is named by exactly 128 rows.
All inputs are finite; a program needn't handle non-finite values.
Results may differ from a plain program's by a relative error of at most 0.018.
Values may be sent and summed in bfloat16 or wider, within the bound.
A program may use at most 320 MiB of HBM per device.

v0:
```python
import jax
import jax.numpy as jnp
from jax import lax
from jax.sharding import PartitionSpec as P

D = 2048
HEAD = 128
TOPK = 8
PROMPT = 256
CONT = 64
GROUP = 384
EPSILON = 1e-05
ROPE_BASE = 10000.0
HIGHEST = lax.Precision.HIGHEST


def matmul(first_op, second_op):
    return jnp.dot(first_op, second_op, preferred_element_type=jnp.float32)


def gather_rows(values):
    return lax.all_gather(values, "tensor", axis=0, tiled=True)


def sum_rows(values):
    return lax.psum_scatter(values, "tensor", scatter_dimension=0, tiled=True)


def tensor_total(values):
    return lax.psum((values[0], values[1]), "tensor")


def expert_swap(values):
    return lax.all_to_all(values, "dp", split_axis=0, concat_axis=0, tiled=True)


def sum_slots(values):
    return lax.psum_scatter(values, "tensor", scatter_dimension=1, tiled=True)


def group_positions():
    position = jnp.arange(GROUP, dtype=jnp.int32)
    return jnp.where(position < PROMPT, position, PROMPT + (position - PROMPT) % CONT)


def visible_keys():
    position = jnp.arange(GROUP, dtype=jnp.int32)
    member = jnp.where(position < PROMPT, -1, (position - PROMPT) // CONT)
    causal = position[None, :] <= position[:, None]
    return causal & ((member[None, :] == -1) | (member[None, :] == member[:, None]))


def rope_tables():
    half_head = HEAD // 2
    frequency = ROPE_BASE ** (-2.0 * jnp.arange(half_head, dtype=jnp.float32) / HEAD)
    angles = group_positions().astype(jnp.float32)[:, None] * frequency[None, :]
    angles = jnp.concatenate([angles, angles], axis=1)
    return (jnp.cos(angles), jnp.sin(angles))


def rotate(values, cosine_table, sine_table):
    half_head = HEAD // 2
    turned = jnp.concatenate([-values[..., half_head:], values[..., :half_head]], axis=-1)
    return values * cosine_table[:, None, :] + turned * sine_table[:, None, :]


def unrotate(values, cosine_table, sine_table):
    half_head = HEAD // 2
    scaled = values * sine_table[:, None, :]
    turned = jnp.concatenate([scaled[..., half_head:], -scaled[..., :half_head]], axis=-1)
    return values * cosine_table[:, None, :] + turned


def gate_split(rows_in, hot_table, router):
    gates = jax.nn.softmax(matmul(rows_in, router), axis=1)
    weights = jnp.sum(jnp.where(hot_table, gates[:, None, :], 0.0), axis=2)
    return (gates, weights)


def body(
    tokens,
    routes,
    cotangent,
    attn_gain,
    q_gain,
    k_gain,
    w_query,
    w_key,
    w_value,
    w_out,
    mlp_gain,
    router,
    w_gate,
    w_up,
    w_down,
):
    rank_index = lax.axis_index("tensor")
    tensor_count = lax.axis_size("tensor")
    own_rows = tokens.shape[0]
    head_cols = w_query.shape[1]
    local_heads = head_cols // HEAD
    col_start = rank_index * head_cols
    row_start = rank_index * own_rows
    experts = router.shape[1]
    half_cap = (own_rows * TOPK * 4 + 3 * experts - 1) // (3 * experts)
    capacity = tensor_count * half_cap
    attn_scale = HEAD ** (-0.5)
    head_shape = (GROUP, local_heads, HEAD)
    q_gain_local = lax.dynamic_slice_in_dim(q_gain, col_start, head_cols)
    k_gain_local = lax.dynamic_slice_in_dim(k_gain, col_start, head_cols)
    inputs = tokens.astype(jnp.float32)
    attn_inv = lax.rsqrt(jnp.mean(inputs * inputs, axis=1, keepdims=True) + EPSILON)
    normed = gather_rows((inputs * attn_inv * attn_gain).astype(jnp.bfloat16))
    pieces = (
        lax.all_gather(w_query, "dp", axis=0, tiled=True),
        lax.all_gather(w_key, "dp", axis=0, tiled=True),
        lax.all_gather(w_value, "dp", axis=0, tiled=True),
    )
    normed_part = normed
    queries = matmul(normed_part, pieces[0])
    keys_raw = matmul(normed_part, pieces[1])
    values_raw = matmul(normed_part, pieces[2])
    query_sq, key_sq = tensor_total(
        (jnp.sum(queries * queries, axis=1), jnp.sum(keys_raw * keys_raw, axis=1))
    )
    query_inv = lax.rsqrt(query_sq / D + EPSILON)[:, None]
    key_inv = lax.rsqrt(key_sq / D + EPSILON)[:, None]
    cosine_table, sine_table = rope_tables()
    query_rot = rotate(
        (queries * query_inv * q_gain_local).reshape(head_shape), cosine_table, sine_table
    ).astype(jnp.bfloat16)
    key_rot = rotate(
        (keys_raw * key_inv * k_gain_local).reshape(head_shape), cosine_table, sine_table
    ).astype(jnp.bfloat16)
    value_heads = values_raw.astype(jnp.bfloat16).reshape(head_shape)
    visible = visible_keys()[None]

    def masked_scores():
        raw_scores = (
            jnp.einsum("qhd,khd->hqk", query_rot, key_rot, preferred_element_type=jnp.float32)
            * attn_scale
        )
        return jnp.where(visible, raw_scores, -1e30)

    scores = masked_scores()
    row_max = jnp.max(scores, axis=2, keepdims=True)
    exponent = jnp.exp(scores - row_max)
    row_total = jnp.sum(exponent, axis=2, keepdims=True)
    log_total = row_max + jnp.log(row_total)
    mixed_heads = jnp.einsum(
        "hqk,khd->qhd",
        (exponent / row_total).astype(jnp.bfloat16),
        value_heads,
        preferred_element_type=jnp.float32,
    )
    mixed_heads = mixed_heads.reshape(GROUP, head_cols).astype(jnp.bfloat16)
    attn_part = matmul(mixed_heads, lax.all_gather(w_out, "dp", axis=1, tiled=True))
    attended = sum_rows(attn_part)
    hidden_one = inputs + attended
    mlp_inv = lax.rsqrt(jnp.mean(hidden_one * hidden_one, axis=1, keepdims=True) + EPSILON)
    normed_two = (hidden_one * mlp_inv * mlp_gain).astype(jnp.bfloat16)
    expert_ids = jnp.arange(experts, dtype=jnp.int32)
    route_hot = routes[:, :, None] == expert_ids[None, None, :]
    flat_hot = route_hot.astype(jnp.int32).reshape(tensor_count, own_rows * TOPK, experts)
    within = jnp.sum((jnp.cumsum(flat_hot, axis=1) - flat_hot) * flat_hot, axis=2).reshape(
        GROUP, TOPK
    )
    owner_of = (jnp.arange(GROUP, dtype=jnp.int32) // own_rows)[:, None]
    own_routes = lax.dynamic_slice_in_dim(routes, row_start, own_rows, 0)
    own_within = lax.dynamic_slice_in_dim(within, row_start, own_rows, 0)
    own_hot = lax.dynamic_slice_in_dim(route_hot, row_start, own_rows, 0)
    own_dest = own_routes * half_cap + own_within
    gate_weight = w_gate[0]
    up_weight = w_up[0]
    down_weight = w_down[0]
    normed_two_all = gather_rows(normed_two)
    gates_every, gate_every = gate_split(normed_two_all, route_hot, router)
    own_probs = lax.dynamic_slice_in_dim(gates_every, row_start, own_rows, 0)
    gate_weights = lax.dynamic_slice_in_dim(gate_every, row_start, own_rows, 0)
    destination = routes * capacity + owner_of * half_cap + within
    send_rows = (
        jnp.zeros((experts * capacity, D), jnp.bfloat16)
        .at[destination]
        .set(jnp.broadcast_to(normed_two_all[:, None, :], (GROUP, TOPK, D)))
        .reshape(experts, capacity, D)
    )
    received = lax.all_to_all(send_rows, "dp", split_axis=0, concat_axis=0, tiled=True)
    gate_pre = jnp.einsum("scd,df->scf", received, gate_weight, preferred_element_type=jnp.float32)
    up_pre = jnp.einsum("scd,df->scf", received, up_weight, preferred_element_type=jnp.float32)
    hidden = (jax.nn.silu(gate_pre) * up_pre).astype(jnp.bfloat16)
    expert_part = jnp.einsum("scf,fd->scd", hidden, down_weight, preferred_element_type=jnp.float32)
    expert_part, gate_pre, up_pre, hidden, received = (
        expert_part,
        gate_pre,
        up_pre,
        hidden,
        received,
    )
    back_rows = expert_swap(sum_slots(expert_part).astype(jnp.bfloat16)).reshape(
        experts * half_cap, D
    )
    picked = back_rows[own_dest].astype(jnp.float32)
    mixture = jnp.sum(gate_weights[:, :, None] * picked, axis=1)
    layer_out = (hidden_one + mixture).astype(jnp.bfloat16)
    upstream = cotangent.astype(jnp.float32)
    gate_grad = jnp.sum(upstream[:, None, :] * picked, axis=2)
    upstream_all = gather_rows(cotangent).astype(jnp.float32)
    send_grads = (
        jnp.zeros((experts * capacity, D), jnp.bfloat16)
        .at[destination]
        .set((gate_every[:, :, None] * upstream_all[:, None, :]).astype(jnp.bfloat16))
        .reshape(experts, capacity, D)
    )
    out_grads = expert_swap(send_grads)
    hidden_grad = jnp.einsum(
        "scd,fd->scf", out_grads, down_weight, preferred_element_type=jnp.float32
    )
    sigmoid = jax.nn.sigmoid(gate_pre)
    up_grad = (hidden_grad * gate_pre * sigmoid).astype(jnp.bfloat16)
    gate_pre_grad = (hidden_grad * up_pre * sigmoid * (1.0 + gate_pre * (1.0 - sigmoid))).astype(
        jnp.bfloat16
    )
    row_part = jnp.einsum(
        "scf,df->scd", gate_pre_grad, gate_weight, preferred_element_type=jnp.float32
    ) + jnp.einsum("scf,df->scd", up_grad, up_weight, preferred_element_type=jnp.float32)
    down_weight_grad = jnp.einsum(
        "scf,scd->fd", hidden, out_grads, preferred_element_type=jnp.float32
    )
    gate_weight_grad = jnp.einsum(
        "scd,scf->df", received, gate_pre_grad, preferred_element_type=jnp.float32
    )
    up_weight_grad = jnp.einsum(
        "scd,scf->df", received, up_grad, preferred_element_type=jnp.float32
    )
    returned_grads = expert_swap(sum_slots(row_part).astype(jnp.bfloat16)).reshape(
        experts * half_cap, D
    )
    normed_two_part = jnp.sum(returned_grads[own_dest].astype(jnp.float32), axis=1)
    expert_grad = jnp.sum(jnp.where(own_hot, gate_grad[:, :, None], 0.0), axis=1)
    logit_grad = own_probs * (expert_grad - jnp.sum(expert_grad * own_probs, axis=1, keepdims=True))
    router_grad = jnp.dot(normed_two.astype(jnp.float32).T, logit_grad, precision=HIGHEST)
    normed_two_grad = normed_two_part + jnp.dot(
        logit_grad, router.astype(jnp.float32).T, precision=HIGHEST
    )
    scaled_grad = normed_two_grad * mlp_gain
    hidden_one_grad = (
        upstream
        + mlp_inv * scaled_grad
        - hidden_one * mlp_inv**3 * jnp.mean(hidden_one * scaled_grad, axis=1, keepdims=True)
    )
    mlp_gain_grad = jnp.sum(normed_two_grad * hidden_one * mlp_inv, axis=0)
    attended_grad = gather_rows(hidden_one_grad.astype(jnp.bfloat16))
    mixed_grad = jnp.einsum(
        "gd,cd->gc",
        attended_grad,
        lax.all_gather(w_out, "dp", axis=1, tiled=True),
        preferred_element_type=jnp.float32,
    )
    mixed_grad = mixed_grad.astype(jnp.bfloat16).reshape(head_shape)
    attn_probs = jnp.exp(masked_scores() - log_total)
    prob_grad = jnp.einsum(
        "qhd,khd->hqk", mixed_grad, value_heads, preferred_element_type=jnp.float32
    )
    row_dot = jnp.sum(prob_grad * attn_probs, axis=2, keepdims=True)
    score_grad = (attn_probs * (prob_grad - row_dot)).astype(jnp.bfloat16)
    query_rot_grad = (
        jnp.einsum("hqk,khd->qhd", score_grad, key_rot, preferred_element_type=jnp.float32)
        * attn_scale
    )
    key_rot_grad = (
        jnp.einsum("hqk,qhd->khd", score_grad, query_rot, preferred_element_type=jnp.float32)
        * attn_scale
    )
    value_grad = (
        jnp.einsum(
            "hqk,qhd->khd",
            attn_probs.astype(jnp.bfloat16),
            mixed_grad,
            preferred_element_type=jnp.float32,
        )
        .reshape(GROUP, head_cols)
        .astype(jnp.bfloat16)
    )
    query_norm_grad = unrotate(query_rot_grad, cosine_table, sine_table).reshape(GROUP, head_cols)
    key_norm_grad = unrotate(key_rot_grad, cosine_table, sine_table).reshape(GROUP, head_cols)
    query_scaled = query_norm_grad * q_gain_local
    key_scaled = key_norm_grad * k_gain_local
    query_dot, key_dot = tensor_total(
        (jnp.sum(queries * query_scaled, axis=1), jnp.sum(keys_raw * key_scaled, axis=1))
    )
    query_grad = (
        query_inv * query_scaled - queries * query_inv**3 * (query_dot / D)[:, None]
    ).astype(jnp.bfloat16)
    key_grad = (key_inv * key_scaled - keys_raw * key_inv**3 * (key_dot / D)[:, None]).astype(
        jnp.bfloat16
    )
    q_gain_part = jnp.sum(query_norm_grad * queries * query_inv, axis=0)
    k_gain_part = jnp.sum(key_norm_grad * keys_raw * key_inv, axis=0)
    pieces = lax.all_gather((w_query, w_key, w_value), "dp", axis=0, tiled=True)
    normed_part = (
        jnp.einsum("gc,rc->gr", query_grad, pieces[0], preferred_element_type=jnp.float32)
        + jnp.einsum("gc,rc->gr", key_grad, pieces[1], preferred_element_type=jnp.float32)
        + jnp.einsum("gc,rc->gr", value_grad, pieces[2], preferred_element_type=jnp.float32)
    )
    weight_sums = lax.psum_scatter(
        jnp.concatenate(
            [
                jnp.einsum("gr,gc->rc", normed, query_grad, preferred_element_type=jnp.float32),
                jnp.einsum("gr,gc->rc", normed, key_grad, preferred_element_type=jnp.float32),
                jnp.einsum("gr,gc->rc", normed, value_grad, preferred_element_type=jnp.float32),
                jnp.einsum(
                    "gr,gc->rc", attended_grad, mixed_heads, preferred_element_type=jnp.float32
                ),
            ],
            axis=1,
        ),
        "dp",
        scatter_dimension=0,
        tiled=True,
    )
    normed_grad = sum_rows(normed_part)
    scaled_input = normed_grad * attn_gain
    tokens_grad = (
        hidden_one_grad
        + attn_inv * scaled_input
        - inputs * attn_inv**3 * jnp.mean(inputs * scaled_input, axis=1, keepdims=True)
    )
    attn_gain_grad = jnp.sum(normed_grad * inputs * attn_inv, axis=0)
    zero_width = jnp.zeros((D,), jnp.float32)
    q_gain_full = lax.dynamic_update_slice_in_dim(zero_width, q_gain_part, col_start, 0)
    k_gain_full = lax.dynamic_update_slice_in_dim(zero_width, k_gain_part, col_start, 0)
    attn_gain_grad, q_gain_grad, k_gain_grad, mlp_gain_grad, router_grad = lax.psum(
        (attn_gain_grad, q_gain_full, k_gain_full, mlp_gain_grad, router_grad), ("dp", "tensor")
    )
    return (
        layer_out,
        tokens_grad,
        attn_gain_grad,
        q_gain_grad,
        k_gain_grad,
        weight_sums[:, :head_cols],
        weight_sums[:, head_cols : 2 * head_cols],
        weight_sums[:, 2 * head_cols : 3 * head_cols],
        jnp.transpose(weight_sums[:, 3 * head_cols :]),
        mlp_gain_grad,
        router_grad,
        gate_weight_grad[None],
        up_weight_grad[None],
        down_weight_grad[None],
    )


def solution(mesh):
    in_specs = (
        P(("dp", "tensor"), None),
        P("dp", None),
        P(("dp", "tensor"), None),
        P(),
        P(),
        P(),
        P("dp", "tensor"),
        P("dp", "tensor"),
        P("dp", "tensor"),
        P("tensor", "dp"),
        P(),
        P(),
        P("dp", None, "tensor"),
        P("dp", None, "tensor"),
        P("dp", "tensor", None),
    )
    out_specs = (
        P(("dp", "tensor"), None),
        P(("dp", "tensor"), None),
        P(),
        P(),
        P(),
        P("dp", "tensor"),
        P("dp", "tensor"),
        P("dp", "tensor"),
        P("tensor", "dp"),
        P(),
        P(),
        P("dp", None, "tensor"),
        P("dp", None, "tensor"),
        P("dp", "tensor", None),
    )
    return jax.shard_map(body, mesh=mesh, in_specs=in_specs, out_specs=out_specs, check_vma=False)
```

profile of v0, /device:TPU:0, one launch (start us, length us, event | category | flops | bytes accessed | tf_op | source)
XLA Modules:
  0.0 2718.6 jit_solution(3922574708786858665)
XLA Ops:
  16.7 25.5 all-gather.9.cloned.1.call-done
  42.2 52.9 %all-gather.15.cloned.1.call-done = bf16[2048,1024]{1,0:T(8,128)(2,1)} async-done(((bf16[128,1024]{1,0:T(8,128)(2,1)}), bf16[2048,1024]{1,0:T(8,128)(2,1)}) %all-gather.15.cloned.1.call-update) | async-done | bytes 4194320 | tf_op jit(solution)/shard_map/all_gather | solution.py:116
  100.7 45.7 %all-gather.13.cloned.1.call-done = bf16[2048,1024]{1,0:T(8,128)(2,1)} async-done(((bf16[128,1024]{1,0:T(8,128)(2,1)}), bf16[2048,1024]{1,0:T(8,128)(2,1)}) %all-gather.13.cloned.1.call-update) | async-done | bytes 4194320 | tf_op jit(solution)/shard_map/all_gather | solution.py:115
  177.6 20.0 all-gather.11.cloned.1.call-done
  204.2 47.0 %all-gather.17.cloned.1.call-done = bf16[1024,2048]{1,0:T(8,128)(2,1)} async-done(((bf16[1024,128]{1,0:T(8,128)(2,1)}), bf16[1024,2048]{1,0:T(8,128)(2,1)}) %all-gather.17.cloned.1.call-update) | async-done | bytes 4194320 | tf_op jit(solution)/shard_map/all_gather | solution.py:157
  257.2 41.4 %reduce-scatter.6.cloned.1.call-done = f32[192,2048]{1,0:T(8,128)} async-done(((f32[384,2048]{1,0:T(8,128)}), f32[192,2048]{1,0:T(8,128)}) %reduce-scatter.6.cloned.1.call-update) | async-done | bytes 1572880 | tf_op jit(solution)/shard_map/reduce_scatter | solution.py:26
  313.4 16.6 all-gather.19.cloned.1.call-done
  330.0 27.6 %scatter_custom_fusion = bf16[4096,2048]{1,0:T(8,128)(2,1)} fusion(s32[3072]{0:T(1024)S(1)} %reshape.372, bf16[]{:T(256)} %constant.98.clone.1, bf16[384,2048]{1,0:T(8,128)(2,1)} %all-gather.19.cloned.1.call-done), kind=kCustom, calls=%fused_computation.14 | custom fusion | bytes 18350082 | tf_op jit(solution)/shard_map/scatter | solution.py:184
  364.1 29.3 %all-gather.21.cloned.1.call-done = bf16[384,2048]{1,0:T(8,128)(2,1)} async-done(((bf16[192,2048]{1,0:T(8,128)(2,1)}), bf16[384,2048]{1,0:T(8,128)(2,1)}) %all-gather.21.cloned.1.call-update) | async-done | bytes 1572880 | tf_op jit(solution)/shard_map/all_gather | solution.py:22
  398.4 28.4 %scatter_custom_fusion.1 = bf16[4096,2048]{1,0:T(8,128)(2,1)} fusion(s32[3072]{0:T(1024)S(1)} %reshape.372, f32[384,2048]{1,0:T(8,128)} %convert_element_type.127, f32[384,8]{1,0:T(8,128)S(1)} %copy.176, bf16[]{:T(256)} %constant.98.clone.1), kind=kCustom, calls=%fused_computation.12 | custom fusion | flops 12582912 | bytes 20119554 | tf_op jit(solution)/shard_map/scatter | solution.py:211
  426.8 233.3 %all-to-all-done = bf16[16,256,2048]{2,1,0:T(8,128)(2,1)} async-done(((bf16[16,256,2048]{2,1,0:T(8,128)(2,1)}), bf16[16,256,2048]{2,1,0:T(8,128)(2,1)}, u32[]{:S(2)}, u32[]{:S(2)}) %all-to-all-start) | async-done | bytes 16777248 | tf_op jit(solution)/shard_map/all_to_all | solution.py:187
  660.1 70.3 %all-to-all-start.2 = ((bf16[16,256,2048]{2,1,0:T(8,128)(2,1)}), bf16[16,256,2048]{2,1,0:T(8,128)(2,1)}, u32[]{:S(2)}, u32[]{:S(2)}) async-start(bf16[16,256,2048]{2,1,0:T(8,128)(2,1)} %bitcast.140), calls=%async_computation.4 | async-start | bytes 33554432 | tf_op jit(solution)/shard_map/all_to_all | solution.py:34
  730.6 15.2 fusion.23
  745.8 14.5 fusion.27
  760.3 266.8 %all-to-all-done.2 = bf16[16,256,2048]{2,1,0:T(8,128)(2,1)} async-done(((bf16[16,256,2048]{2,1,0:T(8,128)(2,1)}), bf16[16,256,2048]{2,1,0:T(8,128)(2,1)}, u32[]{:S(2)}, u32[]{:S(2)}) %all-to-all-start.2) | async-done | bytes 16777248 | tf_op jit(solution)/shard_map/all_to_all | solution.py:34
  1027.2 24.2 multiply_convert_fusion.1
  1051.4 17.9 fusion.25
  1069.3 28.5 %convolution_add_fusion = f32[16,256,2048]{2,1,0:T(8,128)} fusion(f32[16,256,2048]{2,1,0:T(8,128)} %fusion.25, bf16[16,256,512]{2,1,0:T(8,128)(2,1)} %get-tuple-element.106, bf16[1,2048,512]{2,1,0:T(8,128)(2,1)} %param.28), kind=kOutput, calls=%fused_computation.6 | convolution fusion | flops 8598323200 | bytes 73400320 | tf_op jit(solution)/shard_map/scf,df->scd/dot_general | solution.py:225
  1097.8 17.6 fusion.20
  1115.4 416.0 %reduce-scatter.10.cloned.1.call-done = f32[16,128,2048]{2,1,0:T(8,128)} async-done(((f32[16,256,2048]{2,1,0:T(8,128)}), f32[16,128,2048]{2,1,0:T(8,128)}) %reduce-scatter.10.cloned.1.call-update) | async-done | bytes 16777232 | tf_op jit(solution)/shard_map/reduce_scatter | solution.py:38
  1546.2 356.4 %reduce-scatter.8.cloned.1.call-done = f32[16,128,2048]{2,1,0:T(8,128)} async-done(((f32[16,256,2048]{2,1,0:T(8,128)}), f32[16,128,2048]{2,1,0:T(8,128)}) %reduce-scatter.8.cloned.1.call-update) | async-done | bytes 16777232 | tf_op jit(solution)/shard_map/reduce_scatter | solution.py:38
  1919.4 17.3 gather_fusion.1
  1945.6 122.6 %all-to-all-done.1 = bf16[16,128,2048]{2,1,0:T(8,128)(2,1)} async-done(((bf16[16,128,2048]{2,1,0:T(8,128)(2,1)}), bf16[16,128,2048]{2,1,0:T(8,128)(2,1)}, u32[]{:S(2)}, u32[]{:S(2)}) %all-to-all-start.1) | async-done | bytes 8388640 | tf_op jit(solution)/shard_map/all_to_all | solution.py:34
  2068.2 17.1 gather_fusion
  2099.2 58.2 %all-gather.23.cloned.1.call-done = bf16[384,2048]{1,0:T(8,128)(2,1)} async-done(((bf16[192,2048]{1,0:T(8,128)(2,1)}), bf16[384,2048]{1,0:T(8,128)(2,1)}) %all-gather.23.cloned.1.call-update) | async-done | bytes 1572880 | tf_op jit(solution)/shard_map/all_gather | solution.py:22
  2216.1 25.2 pad_maximum_fusion
  2241.6 15.2 convolution_bitcast_fusion
  2256.8 15.6 convolution_bitcast_fusion.1
  2272.4 15.5 convolution_bitcast_fusion.2
  2291.9 42.9 %all-reduce = (f32[2048]{0:T(1024)}, f32[2048]{0:T(1024)}, f32[2048]{0:T(1024)}, f32[2048]{0:T(1024)}) all-reduce(f32[2048]{0:T(1024)S(1)} %get-tuple-element.92, f32[2048]{0:T(1024)S(1)} %dynamic_update_slice.6, f32[2048]{0:T(1024)S(1)} %dynamic_update_slice.7, ...), channel_id=1, replica_groups=mesh['dp'=16,'tensor'=2] {'dp','tensor'}, use_global_device_ids=true, to_apply=%region_33.34 | all-reduce | flops 8192 | bytes 65536 | tf_op jit(solution)/shard_map/psum | solution.py:332
  2338.3 244.4 %reduce-scatter.14.cloned.1.call-done = f32[128,4096]{0,1:T(8,128)} async-done(((f32[2048,4096]{0,1:T(8,128)}), f32[128,4096]{0,1:T(8,128)}) %reduce-scatter.14.cloned.1.call-update) | async-done | bytes 2097168 | tf_op jit(solution)/shard_map/reduce_scatter | solution.py:305
  2589.5 120.7 %all-reduce.5.cloned.1.call-done = f32[2048,16]{0,1:T(8,128)} async-done(((f32[2048,16]{0,1:T(8,128)}), f32[2048,16]{0,1:T(8,128)}) %all-reduce.5.cloned.1.call-update) | async-done | bytes 131088 | tf_op jit(solution)/shard_map/psum | solution.py:332
  (298 shorter events, 213.4 us)
Async XLA Ops:
  7.2 1020.0 %copy-start = (bf16[1,512,2048]{2,1,0:T(8,128)(2,1)S(1)}, bf16[1,512,2048]{2,1,0:T(8,128)(2,1)}, u32[]{:S(2)}) copy-start(bf16[1,512,2048]{2,1,0:T(8,128)(2,1)} %param.29) | copy-start | bytes 6291460
  7.2 35.0 %all-gather.9.cloned.1.call-start = ((), (), s32[]{:S(2)}) async-start(), calls=%async_computation.9 | async-start | bytes 2359296 | tf_op jit(solution)/shard_map/all_gather | solution.py:22
  12.2 83.0 %all-gather.15.cloned.1.call-start = ((), (), s32[]{:S(2)}) async-start(), calls=%async_computation.12 | async-start | bytes 4456448 | tf_op jit(solution)/shard_map/all_gather | solution.py:116
  12.9 133.5 %all-gather.13.cloned.1.call-start = ((), (), s32[]{:S(2)}) async-start(), calls=%async_computation.11 | async-start | bytes 4456448 | tf_op jit(solution)/shard_map/all_gather | solution.py:115
  13.7 183.9 %all-gather.11.cloned.1.call-start = ((), (), s32[]{:S(2)}) async-start(), calls=%async_computation.10 | async-start | bytes 4456448 | tf_op jit(solution)/shard_map/all_gather | solution.py:117
  14.2 237.0 %all-gather.17.cloned.1.call-start = ((), (), s32[]{:S(2)}) async-start(), calls=%async_computation.13 | async-start | bytes 4456448 | tf_op jit(solution)/shard_map/all_gather | solution.py:157
  14.8 283.8 %reduce-scatter.6.cloned.1.call-start = ((), (), s32[]{:S(2)}) async-start(), calls=%async_computation.14 | async-start | bytes 4718592 | tf_op jit(solution)/shard_map/reduce_scatter | solution.py:26
  14.9 149.2 %copy-start.51 = (f32[1024]{0:T(1024)}, f32[1024]{0:T(1024)S(1)}, u32[]{:S(2)}) copy-start(f32[1024]{0:T(1024)S(1)} %dynamic_slice.21) | copy-start | bytes 12292
  14.9 142.8 %copy-start.49 = (f32[1024]{0:T(1024)}, f32[1024]{0:T(1024)S(1)}, u32[]{:S(2)}) copy-start(f32[1024]{0:T(1024)S(1)} %dynamic_slice.22) | copy-start | bytes 12292
  174.8 27.4 %copy-start.42 = (f32[8,384]{1,0:T(8,128)}, f32[8,384]{1,0:T(8,128)S(1)}, u32[]{:S(2)}) copy-start(f32[8,384]{1,0:T(8,128)S(1)} %get-tuple-element.144) | copy-start | bytes 36868
  204.2 47.0 %copy-start.21 = (bf16[8,128,384]{2,1,0:T(8,128)(2,1)}, bf16[8,128,384]{2,1,0:T(8,128)(2,1)S(1)}, u32[]{:S(2)}) copy-start(bf16[8,128,384]{2,1,0:T(8,128)(2,1)S(1)} %fusion.41) | copy-start | bytes 2359300
  256.9 41.7 %copy-start.6 = (bf16[192,2048]{1,0:T(8,128)(2,1)S(1)}, bf16[192,2048]{1,0:T(8,128)(2,1)}, u32[]{:S(2)}) copy-start(bf16[192,2048]{1,0:T(8,128)(2,1)} %param.15) | copy-start | bytes 2359300
  257.0 44.6 %copy-start.47 = (f32[2048]{0:T(1024)S(1)}, f32[2048]{0:T(1024)}, u32[]{:S(2)}) copy-start(f32[2048]{0:T(1024)} %param.25) | copy-start | bytes 24580
  257.0 73.1 %all-gather.19.cloned.1.call-start = ((), (), s32[]{:S(2)}) async-start(), calls=%async_computation.15 | async-start | bytes 2359296 | tf_op jit(solution)/shard_map/all_gather | solution.py:22
  302.8 54.9 %copy-start.28 = (s32[384,8]{1,0:T(8,128)}, s32[384,8]{1,0:T(8,128)S(1)}, u32[]{:S(2)}) copy-start(s32[384,8]{1,0:T(8,128)S(1)} %copy.169) | copy-start | bytes 36868
  313.1 44.6 %copy-start.30 = (s32[384,8]{1,0:T(8,128)}, s32[384,8]{1,0:T(8,128)S(1)}, u32[]{:S(2)}) copy-start(s32[384,8]{1,0:T(8,128)S(1)} %reshape.346) | copy-start | bytes 36868
  357.7 302.4 %all-to-all-start = ((bf16[16,256,2048]{2,1,0:T(8,128)(2,1)}), bf16[16,256,2048]{2,1,0:T(8,128)(2,1)}, u32[]{:S(2)}, u32[]{:S(2)}) async-start(bf16[16,256,2048]{2,1,0:T(8,128)(2,1)} %bitcast.139), calls=%async_computation.1 | async-start | bytes 33554432 | tf_op jit(solution)/shard_map/all_to_all | solution.py:187
  363.4 30.1 %all-gather.21.cloned.1.call-start = ((), (), s32[]{:S(2)}) async-start(), calls=%async_computation.17 | async-start | bytes 2359296 | tf_op jit(solution)/shard_map/all_gather | solution.py:22
  364.1 32.9 %copy-start.38 = (bf16[2048,16]{0,1:T(8,128)(2,1)S(1)}, bf16[2048,16]{0,1:T(8,128)(2,1)}, u32[]{:S(2)}) copy-start(bf16[2048,16]{0,1:T(8,128)(2,1)} %param.26) | copy-start | bytes 196612
  398.3 28.5 %copy-start.44 = (f32[384,8]{0,1:T(8,128)}, f32[384,8]{0,1:T(8,128)S(1)}, u32[]{:S(2)}) copy-start(f32[384,8]{0,1:T(8,128)S(1)} %select_reduce_fusion) | copy-start | bytes 36868
  660.1 367.0 %all-to-all-start.2 = ((bf16[16,256,2048]{2,1,0:T(8,128)(2,1)}), bf16[16,256,2048]{2,1,0:T(8,128)(2,1)}, u32[]{:S(2)}, u32[]{:S(2)}) async-start(bf16[16,256,2048]{2,1,0:T(8,128)(2,1)} %bitcast.140), calls=%async_computation.4 | async-start | bytes 33554432 | tf_op jit(solution)/shard_map/all_to_all | solution.py:34
  730.4 801.0 %reduce-scatter.10.cloned.1.call-start = ((), (), s32[]{:S(2)}) async-start(), calls=%async_computation.18 | async-start | bytes 50331648 | tf_op jit(solution)/shard_map/reduce_scatter | solution.py:38
  1097.8 804.9 %reduce-scatter.8.cloned.1.call-start = ((), (), s32[]{:S(2)}) async-start(), calls=%async_computation.16 | async-start | bytes 50331648 | tf_op jit(solution)/shard_map/reduce_scatter | solution.py:38
  1540.6 371.2 %all-to-all-start.3 = ((bf16[16,128,2048]{2,1,0:T(8,128)(2,1)}), bf16[16,128,2048]{2,1,0:T(8,128)(2,1)}, u32[]{:S(2)}, u32[]{:S(2)}) async-start(bf16[16,128,2048]{2,1,0:T(8,128)(2,1)} %convert_element_type.131), calls=%async_computation.6 | async-start | bytes 16777216 | tf_op jit(solution)/shard_map/all_to_all | solution.py:34
  1911.7 156.5 %all-to-all-start.1 = ((bf16[16,128,2048]{2,1,0:T(8,128)(2,1)}), bf16[16,128,2048]{2,1,0:T(8,128)(2,1)}, u32[]{:S(2)}, u32[]{:S(2)}) async-start(bf16[16,128,2048]{2,1,0:T(8,128)(2,1)} %convert_element_type.123), calls=%async_computation.3 | async-start | bytes 16777216 | tf_op jit(solution)/shard_map/all_to_all | solution.py:34
  1917.6 239.8 %all-gather.23.cloned.1.call-start = ((), (), s32[]{:S(2)}) async-start(), calls=%async_computation.19 | async-start | bytes 2359296 | tf_op jit(solution)/shard_map/all_gather | solution.py:22
  2099.1 190.5 %reduce-scatter.12.cloned.1.call-start = ((), (), s32[]{:S(2)}) async-start(), calls=%async_computation.20 | async-start | bytes 4718592 | tf_op jit(solution)/shard_map/reduce_scatter | solution.py:26
  2165.6 31.9 %copy-start.26 = (bf16[8,128,384]{2,1,0:T(8,128)(2,1)}, bf16[8,128,384]{2,1,0:T(8,128)(2,1)S(1)}, u32[]{:S(2)}) copy-start(bf16[8,128,384]{2,1,0:T(8,128)(2,1)S(1)} %fusion.42) | copy-start | bytes 2359300
  2201.5 381.2 %reduce-scatter.14.cloned.1.call-start = ((), (), s32[]{:S(2)}) async-start(), calls=%async_computation.21 | async-start | bytes 35651584 | tf_op jit(solution)/shard_map/reduce_scatter | solution.py:305
  2241.3 468.9 %all-reduce.5.cloned.1.call-start = ((), (), s32[]{:S(2)}) async-start(), calls=%async_computation.22 | async-start | bytes 262144 | tf_op jit(solution)/shard_map/psum | solution.py:332
  2287.9 46.8 %copy-start.66 = (f32[192]{0:T(256)S(1)}, f32[192]{0:T(256)}, u32[]{:S(2)}) copy-start(f32[192]{0:T(256)} %get-tuple-element.136) | copy-start | bytes 2308
  2582.7 129.1 %copy-start.1 = (bf16[1,512,2048]{2,1,0:T(8,128)(2,1)S(1)}, bf16[1,512,2048]{2,1,0:T(8,128)(2,1)}, u32[]{:S(2)}) copy-start(bf16[1,512,2048]{2,1,0:T(8,128)(2,1)} %param.29) | copy-start | bytes 6291460
  (62 other events, 335.2 us)
Sparse Core Ops, SparseCore 0:
  12.3 29.8 all-gather.8
  44.4 50.7 all-gather.14
  97.3 49.0 all-gather.12
  148.4 49.0 all-gather.10
  199.5 51.7 all-gather.16
  257.1 41.5 reduce-scatter.5
  302.8 27.2 all-gather.18
  365.8 27.5 all-gather.20
  1097.9 433.5 reduce-scatter.9
  1533.7 368.9 reduce-scatter.7
  2099.3 58.0 all-gather.22
  2201.6 43.3 reduce-scatter.11
  2249.2 333.4 reduce-scatter.13
  2588.7 121.4 all-reduce.4
where the time goes:
time: 2720 us
  waiting for transfers between devices  2100 us (77%)
  matrix products  227 us (8%)
  other arithmetic  141 us (5%)
  local copies, waits for them, and re-layouts  93.5 us (3%)
  starting transfers between devices  88.9 us (3%)
  blocking collectives  53.1 us (2%)
    reduce_scatter x2, waiting for transfers between devices, sum_slots(): return lax.psum_scatter(values, 'tensor', scatter_dimension=1, tiled=True)  772 us
    all_to_all x3, waiting for transfers between devices, expert_swap(): return lax.all_to_all(values, 'dp', split_axis=0, concat_axis=0, tiled=True)  389 us
    reduce_scatter x1, waiting for transfers between devices, body(): lax.psum_scatter(jnp.concatenate([jnp.einsum('gr,gc->rc', normed, query_g...  244 us
    all_to_all x1, waiting for transfers between devices, body(): lax.all_to_all(send_rows, 'dp', split_axis=0, concat_axis=0, tiled=True)  233 us
    all_gather x4, waiting for transfers between devices, gather_rows(): return lax.all_gather(values, 'tensor', axis=0, tiled=True)  130 us
    psum x1, waiting for transfers between devices, body(): lax.psum((attn_gain_grad, q_gain_full, k_gain_full, mlp_gain_grad, router...  121 us
    all_to_all x3, starting transfers between devices, expert_swap(): return lax.all_to_all(values, 'dp', split_axis=0, concat_axis=0, tiled=True)  81.7 us
  transfers between devices with their start and end apart: 18, of which 16 were waited for; matrix products, arithmetic and copies ran while one was open for 10% of the time, Pallas kernels for 0%

commit v1 on v0

--- a/solution.py
+++ b/solution.py
@@ -12,6 +12,11 @@
 EPSILON = 1e-05
 ROPE_BASE = 10000.0
 HIGHEST = lax.Precision.HIGHEST
+
+
+def axis_by_axis(value, one, other):
+    partial = lax.psum(value, one)
+    return lax.psum(partial, other)
 
 
 def matmul(first_op, second_op):
@@ -329,8 +334,8 @@
     zero_width = jnp.zeros((D,), jnp.float32)
     q_gain_full = lax.dynamic_update_slice_in_dim(zero_width, q_gain_part, col_start, 0)
     k_gain_full = lax.dynamic_update_slice_in_dim(zero_width, k_gain_part, col_start, 0)
-    attn_gain_grad, q_gain_grad, k_gain_grad, mlp_gain_grad, router_grad = lax.psum(
-        (attn_gain_grad, q_gain_full, k_gain_full, mlp_gain_grad, router_grad), ("dp", "tensor")
+    attn_gain_grad, q_gain_grad, k_gain_grad, mlp_gain_grad, router_grad = axis_by_axis(
+        (attn_gain_grad, q_gain_full, k_gain_full, mlp_gain_grad, router_grad), "tensor", "dp"
     )
     return (
         layer_out,

time: 2720 us -> 2690 us (0.989)
  waiting for transfers between devices: 2100 us -> 2030 us
  blocking collectives: 53.1 us -> 80.8 us
    psum x1 -> x2, waiting for transfers between devices: 121 us -> 82.6 us  [the longest x1 82.6 us: axis_by_axis(): return lax.psum(partial, other)]
    psum x1 -> x2, blocking collectives: 42.9 us -> 70.4 us  [the longest x1 62.6 us: axis_by_axis(): return lax.psum(partial, other)]
    reduce_scatter x1, waiting for transfers between devices: 244 us -> 217 us  [body(): lax.psum_scatter(jnp.concatenate([jnp.einsum('gr,gc->rc', normed, query_g...]
  transfers between devices with their start and end apart: 18 -> 19, of which waited for: 16 -> 16; matrix products, arithmetic and copies ran while one was open for 10% -> 12% of each run, Pallas kernels for 0% -> 0%
where the time goes in v1:
time: 2690 us; the launch traced here: 2680 us
  waiting for transfers between devices  2030 us (75%)
  matrix products  228 us (8%)
  other arithmetic  141 us (5%)
  local copies, waits for them, and re-layouts  93.5 us (3%)
  starting transfers between devices  89.1 us (3%)
  blocking collectives  80.8 us (3%)
    reduce_scatter x2, waiting for transfers between devices, sum_slots(): return lax.psum_scatter(values, 'tensor', scatter_dimension=1, tiled=True)  773 us
    all_to_all x3, waiting for transfers between devices, expert_swap(): return lax.all_to_all(values, 'dp', split_axis=0, concat_axis=0, tiled=True)  390 us
    all_to_all x1, waiting for transfers between devices, body(): lax.all_to_all(send_rows, 'dp', split_axis=0, concat_axis=0, tiled=True)  233 us
    reduce_scatter x1, waiting for transfers between devices, body(): lax.psum_scatter(jnp.concatenate([jnp.einsum('gr,gc->rc', normed, query_g...  217 us
    all_gather x4, waiting for transfers between devices, gather_rows(): return lax.all_gather(values, 'tensor', axis=0, tiled=True)  127 us
    psum x1, waiting for transfers between devices, axis_by_axis(): return lax.psum(partial, other)  82.6 us
    all_to_all x3, starting transfers between devices, expert_swap(): return lax.all_to_all(values, 'dp', split_axis=0, concat_axis=0, tiled=True)  81.7 us
    psum x1, blocking collectives, axis_by_axis(): return lax.psum(partial, other)  62.6 us
  transfers between devices with their start and end apart: 19, of which 16 were waited for; matrix products, arithmetic and copies ran while one was open for 12% of the time, Pallas kernels for 0%

profile of v1, /device:TPU:0, one launch (start us, length us, event | category | flops | bytes accessed | tf_op | source)
XLA Modules:
  0.0 2679.4 jit_solution(13397387430539216478)
XLA Ops:
  16.7 25.5 all-gather.9.cloned.1.call-done
  42.2 52.9 %all-gather.15.cloned.1.call-done = bf16[2048,1024]{1,0:T(8,128)(2,1)} async-done(((bf16[128,1024]{1,0:T(8,128)(2,1)}), bf16[2048,1024]{1,0:T(8,128)(2,1)}) %all-gather.15.cloned.1.call-update) | async-done | bytes 4194320 | tf_op jit(solution)/shard_map/all_gather | solution.py:121
  100.7 45.7 %all-gather.13.cloned.1.call-done = bf16[2048,1024]{1,0:T(8,128)(2,1)} async-done(((bf16[128,1024]{1,0:T(8,128)(2,1)}), bf16[2048,1024]{1,0:T(8,128)(2,1)}) %all-gather.13.cloned.1.call-update) | async-done | bytes 4194320 | tf_op jit(solution)/shard_map/all_gather | solution.py:120
  177.5 19.9 all-gather.11.cloned.1.call-done
  204.2 47.1 %all-gather.17.cloned.1.call-done = bf16[1024,2048]{1,0:T(8,128)(2,1)} async-done(((bf16[1024,128]{1,0:T(8,128)(2,1)}), bf16[1024,2048]{1,0:T(8,128)(2,1)}) %all-gather.17.cloned.1.call-update) | async-done | bytes 4194320 | tf_op jit(solution)/shard_map/all_gather | solution.py:162
  257.2 41.4 %reduce-scatter.6.cloned.1.call-done = f32[192,2048]{1,0:T(8,128)} async-done(((f32[384,2048]{1,0:T(8,128)}), f32[192,2048]{1,0:T(8,128)}) %reduce-scatter.6.cloned.1.call-update) | async-done | bytes 1572880 | tf_op jit(solution)/shard_map/reduce_scatter | solution.py:31
  313.4 16.6 all-gather.19.cloned.1.call-done
  330.0 27.6 %scatter_custom_fusion = bf16[4096,2048]{1,0:T(8,128)(2,1)} fusion(s32[3072]{0:T(1024)S(1)} %reshape.372, bf16[]{:T(256)} %constant.98.clone.1, bf16[384,2048]{1,0:T(8,128)(2,1)} %all-gather.19.cloned.1.call-done), kind=kCustom, calls=%fused_computation.14 | custom fusion | bytes 18350082 | tf_op jit(solution)/shard_map/scatter | solution.py:189
  364.1 29.3 %all-gather.21.cloned.1.call-done = bf16[384,2048]{1,0:T(8,128)(2,1)} async-done(((bf16[192,2048]{1,0:T(8,128)(2,1)}), bf16[384,2048]{1,0:T(8,128)(2,1)}) %all-gather.21.cloned.1.call-update) | async-done | bytes 1572880 | tf_op jit(solution)/shard_map/all_gather | solution.py:27
  398.4 28.4 %scatter_custom_fusion.1 = bf16[4096,2048]{1,0:T(8,128)(2,1)} fusion(s32[3072]{0:T(1024)S(1)} %reshape.372, f32[384,2048]{1,0:T(8,128)} %convert_element_type.127, f32[384,8]{1,0:T(8,128)S(1)} %copy.176, bf16[]{:T(256)} %constant.98.clone.1), kind=kCustom, calls=%fused_computation.12 | custom fusion | flops 12582912 | bytes 20119554 | tf_op jit(solution)/shard_map/scatter | solution.py:216
  426.8 233.3 %all-to-all-done = bf16[16,256,2048]{2,1,0:T(8,128)(2,1)} async-done(((bf16[16,256,2048]{2,1,0:T(8,128)(2,1)}), bf16[16,256,2048]{2,1,0:T(8,128)(2,1)}, u32[]{:S(2)}, u32[]{:S(2)}) %all-to-all-start) | async-done | bytes 16777248 | tf_op jit(solution)/shard_map/all_to_all | solution.py:192
  660.1 70.3 %all-to-all-start.2 = ((bf16[16,256,2048]{2,1,0:T(8,128)(2,1)}), bf16[16,256,2048]{2,1,0:T(8,128)(2,1)}, u32[]{:S(2)}, u32[]{:S(2)}) async-start(bf16[16,256,2048]{2,1,0:T(8,128)(2,1)} %bitcast.140), calls=%async_computation.4 | async-start | bytes 33554432 | tf_op jit(solution)/shard_map/all_to_all | solution.py:39
  730.6 15.2 fusion.23
  745.8 14.4 fusion.27
  760.2 266.9 %all-to-all-done.2 = bf16[16,256,2048]{2,1,0:T(8,128)(2,1)} async-done(((bf16[16,256,2048]{2,1,0:T(8,128)(2,1)}), bf16[16,256,2048]{2,1,0:T(8,128)(2,1)}, u32[]{:S(2)}, u32[]{:S(2)}) %all-to-all-start.2) | async-done | bytes 16777248 | tf_op jit(solution)/shard_map/all_to_all | solution.py:39
  1027.1 24.2 multiply_convert_fusion.1
  1051.3 17.8 fusion.25
  1069.1 28.5 %convolution_add_fusion = f32[16,256,2048]{2,1,0:T(8,128)} fusion(f32[16,256,2048]{2,1,0:T(8,128)} %fusion.25, bf16[16,256,512]{2,1,0:T(8,128)(2,1)} %get-tuple-element.110, bf16[1,2048,512]{2,1,0:T(8,128)(2,1)} %param.28), kind=kOutput, calls=%fused_computation.6 | convolution fusion | flops 8598323200 | bytes 73400320 | tf_op jit(solution)/shard_map/scf,df->scd/dot_general | solution.py:230
  1097.6 17.5 fusion.20
  1115.1 416.2 %reduce-scatter.10.cloned.1.call-done = f32[16,128,2048]{2,1,0:T(8,128)} async-done(((f32[16,256,2048]{2,1,0:T(8,128)}), f32[16,128,2048]{2,1,0:T(8,128)}) %reduce-scatter.10.cloned.1.call-update) | async-done | bytes 16777232 | tf_op jit(solution)/shard_map/reduce_scatter | solution.py:43
  1546.1 356.4 %reduce-scatter.8.cloned.1.call-done = f32[16,128,2048]{2,1,0:T(8,128)} async-done(((f32[16,256,2048]{2,1,0:T(8,128)}), f32[16,128,2048]{2,1,0:T(8,128)}) %reduce-scatter.8.cloned.1.call-update) | async-done | bytes 16777232 | tf_op jit(solution)/shard_map/reduce_scatter | solution.py:43
  1919.2 17.3 gather_fusion.1
  1945.4 122.6 %all-to-all-done.1 = bf16[16,128,2048]{2,1,0:T(8,128)(2,1)} async-done(((bf16[16,128,2048]{2,1,0:T(8,128)(2,1)}), bf16[16,128,2048]{2,1,0:T(8,128)(2,1)}, u32[]{:S(2)}, u32[]{:S(2)}) %all-to-all-start.1) | async-done | bytes 8388640 | tf_op jit(solution)/shard_map/all_to_all | solution.py:39
  2068.1 17.1 gather_fusion
  2101.4 55.8 %all-gather.23.cloned.1.call-done = bf16[384,2048]{1,0:T(8,128)(2,1)} async-done(((bf16[192,2048]{1,0:T(8,128)(2,1)}), bf16[384,2048]{1,0:T(8,128)(2,1)}) %all-gather.23.cloned.1.call-update) | async-done | bytes 1572880 | tf_op jit(solution)/shard_map/all_gather | solution.py:27
  2216.3 25.1 pad_maximum_fusion
  2241.8 15.2 convolution_bitcast_fusion
  2257.0 15.6 convolution_bitcast_fusion.1
  2272.6 15.4 convolution_bitcast_fusion.2
  2298.5 62.6 %all-reduce = (f32[2048]{0:T(1024)}, f32[2048]{0:T(1024)}, f32[2048]{0:T(1024)}, f32[2048]{0:T(1024)}) all-reduce(f32[2048]{0:T(1024)S(1)} %get-tuple-element.98, f32[2048]{0:T(1024)S(1)} %get-tuple-element.99, f32[2048]{0:T(1024)S(1)} %get-tuple-element.100, ...), channel_id=1, replica_groups=mesh['dp'=16,'tensor'=2] {'dp'}, use_global_device_ids=true, to_apply=%region_34.35 | all-reduce | flops 8192 | bytes 65536 | tf_op jit(solution)/shard_map/psum | solution.py:19
  2364.6 217.1 %reduce-scatter.14.cloned.1.call-done = f32[128,4096]{0,1:T(8,128)} async-done(((f32[2048,4096]{0,1:T(8,128)}), f32[128,4096]{0,1:T(8,128)}) %reduce-scatter.14.cloned.1.call-update) | async-done | bytes 2097168 | tf_op jit(solution)/shard_map/reduce_scatter | solution.py:310
  2588.5 82.6 %all-reduce.9.cloned.1.call-done = f32[2048,16]{0,1:T(8,128)} async-done(((f32[2048,16]{0,1:T(8,128)}), f32[2048,16]{0,1:T(8,128)}) %all-reduce.9.cloned.1.call-update) | async-done | bytes 131088 | tf_op jit(solution)/shard_map/psum | solution.py:19
  (300 shorter events, 222.6 us)
Async XLA Ops:
  7.2 1019.9 %copy-start = (bf16[1,512,2048]{2,1,0:T(8,128)(2,1)S(1)}, bf16[1,512,2048]{2,1,0:T(8,128)(2,1)}, u32[]{:S(2)}) copy-start(bf16[1,512,2048]{2,1,0:T(8,128)(2,1)} %param.29) | copy-start | bytes 6291460
  7.2 35.0 %all-gather.9.cloned.1.call-start = ((), (), s32[]{:S(2)}) async-start(), calls=%async_computation.9 | async-start | bytes 2359296 | tf_op jit(solution)/shard_map/all_gather | solution.py:27
  12.1 83.0 %all-gather.15.cloned.1.call-start = ((), (), s32[]{:S(2)}) async-start(), calls=%async_computation.12 | async-start | bytes 4456448 | tf_op jit(solution)/shard_map/all_gather | solution.py:121
  12.9 133.5 %all-gather.13.cloned.1.call-start = ((), (), s32[]{:S(2)}) async-start(), calls=%async_computation.11 | async-start | bytes 4456448 | tf_op jit(solution)/shard_map/all_gather | solution.py:120
  13.6 183.9 %all-gather.11.cloned.1.call-start = ((), (), s32[]{:S(2)}) async-start(), calls=%async_computation.10 | async-start | bytes 4456448 | tf_op jit(solution)/shard_map/all_gather | solution.py:122
  14.2 237.0 %all-gather.17.cloned.1.call-start = ((), (), s32[]{:S(2)}) async-start(), calls=%async_computation.13 | async-start | bytes 4456448 | tf_op jit(solution)/shard_map/all_gather | solution.py:162
  14.8 283.8 %reduce-scatter.6.cloned.1.call-start = ((), (), s32[]{:S(2)}) async-start(), calls=%async_computation.14 | async-start | bytes 4718592 | tf_op jit(solution)/shard_map/reduce_scatter | solution.py:31
  14.9 149.2 %copy-start.50 = (f32[1024]{0:T(1024)}, f32[1024]{0:T(1024)S(1)}, u32[]{:S(2)}) copy-start(f32[1024]{0:T(1024)S(1)} %dynamic_slice.21) | copy-start | bytes 12292
  14.9 142.8 %copy-start.48 = (f32[1024]{0:T(1024)}, f32[1024]{0:T(1024)S(1)}, u32[]{:S(2)}) copy-start(f32[1024]{0:T(1024)S(1)} %dynamic_slice.22) | copy-start | bytes 12292
  204.2 47.1 %copy-start.20 = (bf16[8,128,384]{2,1,0:T(8,128)(2,1)}, bf16[8,128,384]{2,1,0:T(8,128)(2,1)S(1)}, u32[]{:S(2)}) copy-start(bf16[8,128,384]{2,1,0:T(8,128)(2,1)S(1)} %fusion.41) | copy-start | bytes 2359300
  256.9 41.7 %copy-start.6 = (bf16[192,2048]{1,0:T(8,128)(2,1)S(1)}, bf16[192,2048]{1,0:T(8,128)(2,1)}, u32[]{:S(2)}) copy-start(bf16[192,2048]{1,0:T(8,128)(2,1)} %param.15) | copy-start | bytes 2359300
  256.9 44.6 %copy-start.46 = (f32[2048]{0:T(1024)S(1)}, f32[2048]{0:T(1024)}, u32[]{:S(2)}) copy-start(f32[2048]{0:T(1024)} %param.25) | copy-start | bytes 24580
  256.9 73.1 %all-gather.19.cloned.1.call-start = ((), (), s32[]{:S(2)}) async-start(), calls=%async_computation.15 | async-start | bytes 2359296 | tf_op jit(solution)/shard_map/all_gather | solution.py:27
  302.8 54.9 %copy-start.27 = (s32[384,8]{1,0:T(8,128)}, s32[384,8]{1,0:T(8,128)S(1)}, u32[]{:S(2)}) copy-start(s32[384,8]{1,0:T(8,128)S(1)} %copy.169) | copy-start | bytes 36868
  313.0 44.6 %copy-start.29 = (s32[384,8]{1,0:T(8,128)}, s32[384,8]{1,0:T(8,128)S(1)}, u32[]{:S(2)}) copy-start(s32[384,8]{1,0:T(8,128)S(1)} %reshape.346) | copy-start | bytes 36868
  357.6 302.4 %all-to-all-start = ((bf16[16,256,2048]{2,1,0:T(8,128)(2,1)}), bf16[16,256,2048]{2,1,0:T(8,128)(2,1)}, u32[]{:S(2)}, u32[]{:S(2)}) async-start(bf16[16,256,2048]{2,1,0:T(8,128)(2,1)} %bitcast.139), calls=%async_computation.1 | async-start | bytes 33554432 | tf_op jit(solution)/shard_map/all_to_all | solution.py:192
  363.3 30.1 %all-gather.21.cloned.1.call-start = ((), (), s32[]{:S(2)}) async-start(), calls=%async_computation.17 | async-start | bytes 2359296 | tf_op jit(solution)/shard_map/all_gather | solution.py:27
  364.1 32.9 %copy-start.37 = (bf16[2048,16]{0,1:T(8,128)(2,1)S(1)}, bf16[2048,16]{0,1:T(8,128)(2,1)}, u32[]{:S(2)}) copy-start(bf16[2048,16]{0,1:T(8,128)(2,1)} %param.26) | copy-start | bytes 196612
  398.2 28.5 %copy-start.43 = (f32[384,8]{0,1:T(8,128)}, f32[384,8]{0,1:T(8,128)S(1)}, u32[]{:S(2)}) copy-start(f32[384,8]{0,1:T(8,128)S(1)} %select_reduce_fusion) | copy-start | bytes 36868
  660.1 367.0 %all-to-all-start.2 = ((bf16[16,256,2048]{2,1,0:T(8,128)(2,1)}), bf16[16,256,2048]{2,1,0:T(8,128)(2,1)}, u32[]{:S(2)}, u32[]{:S(2)}) async-start(bf16[16,256,2048]{2,1,0:T(8,128)(2,1)} %bitcast.140), calls=%async_computation.4 | async-start | bytes 33554432 | tf_op jit(solution)/shard_map/all_to_all | solution.py:39
  730.4 800.9 %reduce-scatter.10.cloned.1.call-start = ((), (), s32[]{:S(2)}) async-start(), calls=%async_computation.18 | async-start | bytes 50331648 | tf_op jit(solution)/shard_map/reduce_scatter | solution.py:43
  1097.6 804.9 %reduce-scatter.8.cloned.1.call-start = ((), (), s32[]{:S(2)}) async-start(), calls=%async_computation.16 | async-start | bytes 50331648 | tf_op jit(solution)/shard_map/reduce_scatter | solution.py:43
  1540.4 371.2 %all-to-all-start.3 = ((bf16[16,128,2048]{2,1,0:T(8,128)(2,1)}), bf16[16,128,2048]{2,1,0:T(8,128)(2,1)}, u32[]{:S(2)}, u32[]{:S(2)}) async-start(bf16[16,128,2048]{2,1,0:T(8,128)(2,1)} %convert_element_type.131), calls=%async_computation.6 | async-start | bytes 16777216 | tf_op jit(solution)/shard_map/all_to_all | solution.py:39
  1911.5 156.5 %all-to-all-start.1 = ((bf16[16,128,2048]{2,1,0:T(8,128)(2,1)}), bf16[16,128,2048]{2,1,0:T(8,128)(2,1)}, u32[]{:S(2)}, u32[]{:S(2)}) async-start(bf16[16,128,2048]{2,1,0:T(8,128)(2,1)} %convert_element_type.123), calls=%async_computation.3 | async-start | bytes 16777216 | tf_op jit(solution)/shard_map/all_to_all | solution.py:39
  1917.4 239.8 %all-gather.23.cloned.1.call-start = ((), (), s32[]{:S(2)}) async-start(), calls=%async_computation.19 | async-start | bytes 2359296 | tf_op jit(solution)/shard_map/all_gather | solution.py:27
  2098.9 189.1 %all-reduce.7.cloned.1.call-start = ((), (), s32[]{:S(2)}) async-start(), calls=%async_computation.22 | async-start | bytes 262144 | tf_op jit(solution)/shard_map/psum | solution.py:18
  2101.3 187.3 %reduce-scatter.12.cloned.1.call-start = ((), (), s32[]{:S(2)}) async-start(), calls=%async_computation.20 | async-start | bytes 4718592 | tf_op jit(solution)/shard_map/reduce_scatter | solution.py:31
  2165.4 32.2 %copy-start.25 = (bf16[8,128,384]{2,1,0:T(8,128)(2,1)}, bf16[8,128,384]{2,1,0:T(8,128)(2,1)S(1)}, u32[]{:S(2)}) copy-start(bf16[8,128,384]{2,1,0:T(8,128)(2,1)S(1)} %fusion.42) | copy-start | bytes 2359300
  2201.6 380.2 %reduce-scatter.14.cloned.1.call-start = ((), (), s32[]{:S(2)}) async-start(), calls=%async_computation.21 | async-start | bytes 35651584 | tf_op jit(solution)/shard_map/reduce_scatter | solution.py:310
  2241.5 429.6 %all-reduce.9.cloned.1.call-start = ((), (), s32[]{:S(2)}) async-start(), calls=%async_computation.23 | async-start | bytes 262144 | tf_op jit(solution)/shard_map/psum | solution.py:19
  2288.0 73.2 %copy-start.65 = (f32[192]{0:T(256)S(1)}, f32[192]{0:T(256)}, u32[]{:S(2)}) copy-start(f32[192]{0:T(256)} %get-tuple-element.140) | copy-start | bytes 2308
  2581.7 90.9 %copy-start.1 = (bf16[1,512,2048]{2,1,0:T(8,128)(2,1)S(1)}, bf16[1,512,2048]{2,1,0:T(8,128)(2,1)}, u32[]{:S(2)}) copy-start(bf16[1,512,2048]{2,1,0:T(8,128)(2,1)} %param.29) | copy-start | bytes 6291460
  (62 other events, 343.7 us)
Sparse Core Ops, SparseCore 0:
  12.2 29.8 all-gather.8
  44.4 50.7 all-gather.14
  97.3 49.0 all-gather.12
  148.4 49.0 all-gather.10
  199.5 51.7 all-gather.16
  257.1 41.5 reduce-scatter.5
  302.7 27.2 all-gather.18
  365.8 27.5 all-gather.20
  1097.7 433.5 reduce-scatter.9
  1533.5 368.8 reduce-scatter.7
  2099.0 58.0 all-gather.22
  2160.0 21.4 all-reduce.6
  2201.7 43.3 reduce-scatter.11
  2249.2 332.4 reduce-scatter.13
  2585.0 86.0 all-reduce.8
